TPU v7x, 32 devices: a whole 2x2x4 slice. The times are simulated.
32 devices in a mesh: dp: 8 (over y, x, core), tensor: 4 (over z).
Axes of the slice: x: 2, y: 2, z: 4, core: 2. Of those that a mesh axis runs over, the one named last changes fastest.
Arguments:
- inputs: bfloat16 [64, 256, 1152], P('dp'), may hold values from -6 to 6
- cotangent: bfloat16 [64, 256, 1152], P('dp'), may hold values from -6 to 6
- counts: int32 [8], P('dp'), may hold values from 1 to 8, as said below
- time_ids: int32 [64], P('dp'), may hold values from 0 to 999
- class_ids: int32 [64], P('dp'), may hold values from 0 to 1000
- time_table: bfloat16 [1000, 1152], replicated, may hold values from -4 to 4
- class_table: bfloat16 [1001, 1152], replicated, may hold values from -4 to 4
- ada_weight: bfloat16 [1152, 6, 1152], P(None, None, 'tensor'), may hold values from -0.1875 to 0.1875
- ada_bias: bfloat16 [6, 1152], P(None, 'tensor'), may hold values from -1.75 to 1.75
- qkv_weight: bfloat16 [1152, 3, 1152], P(None, None, 'tensor'), may hold values from -0.1875 to 0.1875
- qv_bias: bfloat16 [2, 1152], P(None, 'tensor'), may hold values from -1.75 to 1.75
- proj_weight: bfloat16 [1152, 1152], P('tensor'), may hold values from -1.5 to 1.5
- proj_bias: bfloat16 [1152], replicated, may hold values from -1.75 to 1.75
- up_weight: bfloat16 [1152, 4608], P(None, 'tensor'), may hold values from -0.1875 to 0.1875
- up_bias: bfloat16 [4608], P('tensor'), may hold values from -1.75 to 1.75
- down_weight: bfloat16 [4608, 1152], P('tensor'), may hold values from -0.09375 to 0.09375
- down_bias: bfloat16 [1152], replicated, may hold values from -1.75 to 1.75
Outputs:
- outputs: bfloat16 [64, 256, 1152], P('dp')
- grad_inputs: bfloat16 [64, 256, 1152], P('dp')
- grad_time_table: float32 [1000, 1152], replicated
- grad_class_table: float32 [1001, 1152], replicated
- grad_ada_weight: float32 [1152, 6, 1152], P(None, None, 'tensor')
- grad_ada_bias: float32 [6, 1152], P(None, 'tensor')
- grad_qkv_weight: float32 [1152, 3, 1152], P(None, None, 'tensor')
- grad_qv_bias: float32 [2, 1152], P(None, 'tensor')
- grad_proj_weight: float32 [1152, 1152], P('tensor')
- grad_proj_bias: float32 [1152], replicated
- grad_up_weight: float32 [1152, 4608], P(None, 'tensor')
- grad_up_bias: float32 [4608], P('tensor')
- grad_down_weight: float32 [4608, 1152], P('tensor')
- grad_down_bias: float32 [1152], replicated
Inputs may be any that keep to these rules, and one draw needn't show every extreme that they name: Each index of dp holds 8 image slots whose first counts live; at least one index has all 8 live.
All inputs are finite; a program needn't handle non-finite values.
Results may differ from a plain program's by a relative error of at most 0.014.
The roundings to bfloat16 on the way count: a program that leaves them out, or rounds other values in their place, can miss the bound.
Values sent between devices are 32-bit elements; how exact they have to be, the bound alone decides.
No kernel may reach another device: no remote copies, remote signals or barrier semaphores. Data moves between devices by JAX's collectives and lax.ppermute only.
A program may use at most 256 MiB of HBM per device.

v0:
```python
import jax
import jax.numpy as jnp
from jax import lax
from jax.sharding import PartitionSpec as P

HEAD_DIM = 72
EPSILON = 1e-06
GELU_ROOT = 0.7978845608028654
GELU_CUBIC = 0.044715


def norm_parts(values):
    average = jnp.mean(values, axis=-1, keepdims=True)
    centred = values - average
    spread = jnp.mean(centred * centred, axis=-1, keepdims=True)
    inverse = lax.rsqrt(spread + EPSILON)
    return (centred * inverse, inverse)


def norm_back(upstream, normed, inverse):
    first_mean = jnp.mean(upstream, axis=-1, keepdims=True)
    second_mean = jnp.mean(upstream * normed, axis=-1, keepdims=True)
    return inverse * (upstream - first_mean - normed * second_mean)


def gelu_parts(values):
    argument = GELU_ROOT * (values + GELU_CUBIC * values * values * values)
    tangent = jnp.tanh(argument)
    result = 0.5 * values * (1.0 + tangent)
    derivative = 0.5 * (1.0 + tangent) + 0.5 * values * (1.0 - tangent * tangent) * GELU_ROOT * (
        1.0 + 3.0 * GELU_CUBIC * values * values
    )
    return (result, derivative)


def local(
    inputs,
    cotangent,
    counts,
    time_ids,
    class_ids,
    time_table,
    class_table,
    ada_weight,
    ada_bias,
    qkv_weight,
    qv_bias,
    proj_weight,
    proj_bias,
    up_weight,
    up_bias,
    down_weight,
    down_bias,
):
    wide = jnp.float32
    narrow = jnp.bfloat16
    images, length, width = inputs.shape
    local_width = qkv_weight.shape[2]
    heads_here = local_width // HEAD_DIM
    scaling = HEAD_DIM ** (-0.5)
    live = (jnp.arange(images, dtype=jnp.int32) < counts[0]).astype(wide)
    time_levels = jnp.arange(time_table.shape[0], dtype=jnp.int32)
    class_levels = jnp.arange(class_table.shape[0], dtype=jnp.int32)
    time_pick = (time_ids[:, None] == time_levels[None, :]).astype(narrow)
    class_pick = (class_ids[:, None] == class_levels[None, :]).astype(narrow)
    condition = jnp.dot(time_pick, time_table, preferred_element_type=wide) + jnp.dot(
        class_pick, class_table, preferred_element_type=wide
    )
    silu_cond = jax.nn.silu(condition).astype(narrow)
    mod_local = jnp.einsum(
        "gd,dke->gke", silu_cond, ada_weight, preferred_element_type=wide
    ) + ada_bias.astype(wide)
    modulation = lax.all_gather(mod_local, "tensor", axis=2, tiled=True)
    shift_attn = modulation[:, 0, None, :]
    scale_attn = modulation[:, 1, None, :]
    gate_attn = modulation[:, 2, None, :]
    shift_mlp = modulation[:, 3, None, :]
    scale_mlp = modulation[:, 4, None, :]
    gate_mlp = modulation[:, 5, None, :]
    input_wide = inputs.astype(wide)
    normed_attn, inverse_attn = norm_parts(input_wide)
    hidden_attn = (normed_attn * (1.0 + scale_attn) + shift_attn).astype(narrow)
    projected = jnp.einsum("gsd,dke->gske", hidden_attn, qkv_weight, preferred_element_type=wide)
    bias_wide = qv_bias.astype(wide)
    shape_heads = (images, length, heads_here, HEAD_DIM)
    query_heads = (projected[:, :, 0] + bias_wide[0]).astype(narrow).reshape(shape_heads)
    key_heads = projected[:, :, 1].astype(narrow).reshape(shape_heads)
    value_heads = (projected[:, :, 2] + bias_wide[1]).astype(narrow).reshape(shape_heads)
    scores = (
        jnp.einsum("gqhe,gkhe->ghqk", query_heads, key_heads, preferred_element_type=wide) * scaling
    )
    highest = jnp.max(scores, axis=-1, keepdims=True)
    exponent = jnp.exp(scores - highest)
    denominator = jnp.sum(exponent, axis=-1, keepdims=True)
    soft_probs = (exponent / denominator).astype(narrow)
    log_total = highest + jnp.log(denominator)
    heads_out = jnp.einsum("ghqk,gkhe->gqhe", soft_probs, value_heads, preferred_element_type=wide)
    heads_out = heads_out.reshape(images, length, local_width).astype(narrow)
    attn_part = jnp.einsum("gse,ed->gsd", heads_out, proj_weight, preferred_element_type=wide)
    attention = lax.psum(attn_part, "tensor") + proj_bias.astype(wide)
    middle = input_wide + gate_attn * attention
    normed_mlp, inverse_mlp = norm_parts(middle)
    hidden_mlp = (normed_mlp * (1.0 + scale_mlp) + shift_mlp).astype(narrow)
    pre_act = jnp.einsum(
        "gsd,df->gsf", hidden_mlp, up_weight, preferred_element_type=wide
    ) + up_bias.astype(wide)
    gelu_value, gelu_slope = gelu_parts(pre_act)
    activated = gelu_value.astype(narrow)
    mlp_part = jnp.einsum("gsf,fd->gsd", activated, down_weight, preferred_element_type=wide)
    branch = lax.psum(mlp_part, "tensor") + down_bias.astype(wide)
    outputs = ((middle + gate_mlp * branch) * live[:, None, None]).astype(narrow)
    grad_out = cotangent.astype(wide) * live[:, None, None]
    d_gate_mlp = jnp.sum(grad_out * branch, axis=1)
    d_branch = (gate_mlp * grad_out).astype(narrow)
    grad_down_bias = jnp.sum(d_branch, axis=(0, 1), dtype=wide)
    grad_down_weight = jnp.einsum("gsf,gsd->fd", activated, d_branch, preferred_element_type=wide)
    d_activated = jnp.einsum("gsd,fd->gsf", d_branch, down_weight, preferred_element_type=wide)
    d_pre = (d_activated * gelu_slope).astype(narrow)
    grad_up_bias = jnp.sum(d_pre, axis=(0, 1), dtype=wide)
    grad_up_weight = jnp.einsum("gsd,gsf->df", hidden_mlp, d_pre, preferred_element_type=wide)
    grad_down_weight, grad_down_bias, grad_up_weight, grad_up_bias = lax.psum(
        (grad_down_weight, grad_down_bias, grad_up_weight, grad_up_bias), "dp"
    )
    d_mlp_part = jnp.einsum("gsf,df->gsd", d_pre, up_weight, preferred_element_type=wide)
    d_hidden_mlp = lax.psum(d_mlp_part, "tensor")
    d_shift_mlp = jnp.sum(d_hidden_mlp, axis=1)
    d_scale_mlp = jnp.sum(d_hidden_mlp * normed_mlp, axis=1)
    d_middle = grad_out + norm_back(d_hidden_mlp * (1.0 + scale_mlp), normed_mlp, inverse_mlp)
    d_gate_attn = jnp.sum(d_middle * attention, axis=1)
    d_attention = (gate_attn * d_middle).astype(narrow)
    grad_proj_bias = jnp.sum(d_attention, axis=(0, 1), dtype=wide)
    grad_proj_weight = jnp.einsum(
        "gse,gsd->ed", heads_out, d_attention, preferred_element_type=wide
    )
    d_heads = jnp.einsum("gsd,ed->gse", d_attention, proj_weight, preferred_element_type=wide)
    d_heads = d_heads.astype(narrow).reshape(shape_heads)
    scores_again = (
        jnp.einsum("gqhe,gkhe->ghqk", query_heads, key_heads, preferred_element_type=wide) * scaling
    )
    probs_again = jnp.exp(scores_again - log_total)
    d_value = jnp.einsum(
        "ghqk,gqhe->gkhe", probs_again.astype(narrow), d_heads, preferred_element_type=wide
    )
    d_value = d_value.astype(narrow)
    d_probs = jnp.einsum("gqhe,gkhe->ghqk", d_heads, value_heads, preferred_element_type=wide)
    row_inner = jnp.sum(probs_again * d_probs, axis=-1, keepdims=True)
    d_scores = (probs_again * (d_probs - row_inner)).astype(narrow)
    d_query = (
        jnp.einsum("ghqk,gkhe->gqhe", d_scores, key_heads, preferred_element_type=wide) * scaling
    ).astype(narrow)
    d_key = (
        jnp.einsum("ghqk,gqhe->gkhe", d_scores, query_heads, preferred_element_type=wide) * scaling
    ).astype(narrow)
    d_projected = jnp.stack([d_query, d_key, d_value], axis=2).reshape(
        images, length, 3, local_width
    )
    grad_qv_bias = jnp.stack(
        [
            jnp.sum(d_query, axis=(0, 1), dtype=wide).reshape(local_width),
            jnp.sum(d_value, axis=(0, 1), dtype=wide).reshape(local_width),
        ],
        axis=0,
    )
    grad_qkv_weight = jnp.einsum(
        "gsd,gske->dke", hidden_attn, d_projected, preferred_element_type=wide
    )
    d_attn_part = jnp.einsum("gske,dke->gsd", d_projected, qkv_weight, preferred_element_type=wide)
    d_hidden_attn = lax.psum(d_attn_part, "tensor")
    d_shift_attn = jnp.sum(d_hidden_attn, axis=1)
    d_scale_attn = jnp.sum(d_hidden_attn * normed_attn, axis=1)
    grad_inputs = (
        d_middle + norm_back(d_hidden_attn * (1.0 + scale_attn), normed_attn, inverse_attn)
    ).astype(narrow)
    d_modulation = jnp.stack(
        [d_shift_attn, d_scale_attn, d_gate_attn, d_shift_mlp, d_scale_mlp, d_gate_mlp], axis=1
    ).astype(narrow)
    start_column = lax.axis_index("tensor") * local_width
    d_mod_local = lax.dynamic_slice_in_dim(d_modulation, start_column, local_width, 2)
    grad_ada_weight = jnp.einsum("gd,gke->dke", silu_cond, d_mod_local, preferred_element_type=wide)
    grad_ada_bias = jnp.sum(d_mod_local, axis=0, dtype=wide)
    (
        grad_qkv_weight,
        grad_qv_bias,
        grad_proj_weight,
        grad_proj_bias,
        grad_ada_weight,
        grad_ada_bias,
    ) = lax.psum(
        (
            grad_qkv_weight,
            grad_qv_bias,
            grad_proj_weight,
            grad_proj_bias,
            grad_ada_weight,
            grad_ada_bias,
        ),
        "dp",
    )
    sigmoid_cond = jax.nn.sigmoid(condition)
    d_condition = jnp.einsum("gke,dke->gd", d_mod_local, ada_weight, preferred_element_type=wide)
    d_condition = d_condition * sigmoid_cond * (1.0 + condition * (1.0 - sigmoid_cond))
    exact = lax.Precision.HIGHEST
    grad_time_table = jnp.dot(time_pick.astype(wide).T, d_condition, precision=exact)
    grad_class_table = jnp.dot(class_pick.astype(wide).T, d_condition, precision=exact)
    grad_time_table, grad_class_table = lax.psum(
        (grad_time_table, grad_class_table), ("dp", "tensor")
    )
    return (
        outputs,
        grad_inputs,
        grad_time_table,
        grad_class_table,
        grad_ada_weight,
        grad_ada_bias,
        grad_qkv_weight,
        grad_qv_bias,
        grad_proj_weight,
        grad_proj_bias,
        grad_up_weight,
        grad_up_bias,
        grad_down_weight,
        grad_down_bias,
    )


def solution(mesh):
    in_specs = (
        P("dp", None, None),
        P("dp", None, None),
        P("dp"),
        P("dp"),
        P("dp"),
        P(),
        P(),
        P(None, None, "tensor"),
        P(None, "tensor"),
        P(None, None, "tensor"),
        P(None, "tensor"),
        P("tensor", None),
        P(),
        P(None, "tensor"),
        P("tensor"),
        P("tensor", None),
        P(),
    )
    out_specs = (
        P("dp", None, None),
        P("dp", None, None),
        P(),
        P(),
        P(None, None, "tensor"),
        P(None, "tensor"),
        P(None, None, "tensor"),
        P(None, "tensor"),
        P("tensor", None),
        P(),
        P(None, "tensor"),
        P("tensor"),
        P("tensor", None),
        P(),
    )
    return jax.shard_map(local, mesh=mesh, in_specs=in_specs, out_specs=out_specs, check_vma=False)
```

profile of v0, /device:TPU:0, one launch (start us, length us, event | category | flops | bytes accessed | tf_op | source)
XLA Modules:
  0.0 2098.7 jit_solution(2705256795855632784)
XLA Ops:
  7.3 3.2 convert_reduce_fusion
  10.5 4.5 fusion.14
  16.7 1.3 convolution_add_fusion.1
  18.0 1.5 copy.58
  19.4 91.1 %all_gather.3 = f32[8,6,1152]{1,0,2:T(8,128)} all-gather(f32[8,6,288]{1,0,2:T(8,128)} %copy.58), channel_id=1, replica_groups=mesh['dp'=8,'tensor'=4] {'tensor'}, dimensions={2}, use_global_device_ids=true | all-gather | bytes 276480 | tf_op jit(solution)/shard_map/all_gather | solution.py:73
  110.5 22.1 %fusion.73 = (f32[8,1,1152]{1,0,2:T(8,128)}, f32[8,1,1152]{1,0,2:T(8,128)}, f32[8,1,1152]{1,0,2:T(8,128)}, f32[8,1,1152]{1,0,2:T(8,128)}, f32[8,1,1152]{1,0,2:T(8,128)}, /*index=5*/f32[8,1,1152]{1,0,2:T(8,128)}) fusion(f32[8,6,1152]{1,0,2:T(8,128)} %all_gather.3), kind=kLoop, calls=%fused_computation.140 | loop fusion | bytes 442368 | tf_op jit(solution)/shard_map/slice | solution.py:79
  132.6 3.3 copy.86
  135.9 3.3 copy.85
  139.3 7.8 fusion.40
  147.2 1.1 slice.59
  148.3 2.7 fusion.72
  151.2 3.5 multiply_reduce_fusion.8
  154.7 1.6 fusion.22
  156.4 2.2 fusion.42
  158.6 1.0 copy-done.17
  159.6 5.4 fusion.49
  165.7 3.3 copy.87
  169.1 3.6 copy.88
  172.7 3.3 copy.84
  176.1 3.9 copy.89
  180.0 310.3 %all-reduce.10.cloned.1.call-done = f32[8,256,1152]{2,1,0:T(8,128)} async-done(((f32[8,256,1152]{2,1,0:T(8,128)}), f32[8,256,1152]{2,1,0:T(8,128)}) %all-reduce.10.cloned.1.call-update) | async-done | bytes 9437200 | tf_op jit(solution)/shard_map/psum | solution.py:100
  490.3 10.4 fusion.71
  500.7 4.9 multiply_reduce_fusion.4
  505.7 1.4 copy-done.2
  507.1 9.6 fusion.35
  516.7 12.8 convert_reduce_fusion.2
  529.5 2.3 copy-done.59
  531.8 9.6 fusion.33
  542.2 13.1 fusion.31
  555.3 309.9 %all-reduce.12.cloned.1.call-done = f32[8,256,1152]{2,1,0:T(8,128)} async-done(((f32[8,256,1152]{2,1,0:T(8,128)}), f32[8,256,1152]{2,1,0:T(8,128)}) %all-reduce.12.cloned.1.call-update) | async-done | bytes 9437200 | tf_op jit(solution)/shard_map/psum | solution.py:125
  865.2 8.5 multiply_reduce_fusion.1
  874.4 11.4 convert_reduce_fusion.3
  885.8 1.7 convolution_convert_fusion
  888.2 1.5 slice-done
  889.7 1.3 slice-done.1
  891.0 1.8 convert_reduce_fusion.4
  892.8 2.6 multiply_reduce_fusion.5
  895.4 2.5 multiply_convert_fusion.4
  897.9 1.4 multiply_convert_fusion.5
  899.4 1.0 convert_reduce_fusion.5
  900.4 7.9 convolution_bitcast_fusion.2
  909.1 16.6 convolution_bitcast_fusion
  925.7 611.2 %all-reduce.18.cloned.1.call-done = (f32[8,256,1152]{2,1,0:T(8,128)}, f32[8,256,1152]{2,1,0:T(8,128)}) async-done(((f32[8,256,1152]{2,1,0:T(8,128)}, f32[8,256,1152]{2,1,0:T(8,128)}), (f32[8,256,1152]{2,1,0:T(8,128)}, f32[8,256,1152]{2,1,0:T(8,128)})) %all-reduce.18.cloned.1.call-update) | async-done | bytes 18874384 | tf_op jit(solution)/shard_map/psum | solution.py:110
  1537.0 8.8 fusion.13
  1545.9 13.2 convert_reduce_fusion.1
  1559.3 9.1 multiply_reduce_fusion.2
  1569.2 4.4 fusion.54
  1573.6 4.3 fusion.53
  1578.4 15.1 convolution_bitcast_fusion.1
  1593.5 5.3 convolution_bitcast_fusion.4
  1598.8 9.8 convolution_bitcast_fusion.3
  1608.6 4.7 fusion.56
  1614.0 24.1 %all-reduce.1 = (f32[6,288]{1,0:T(8,128)}, f32[2,288]{1,0:T(2,128)}, f32[1152]{0:T(1024)}, f32[1152]{0:T(1024)}, f32[1152]{0:T(1024)}) all-reduce(f32[6,288]{1,0:T(8,128)S(1)} %convert_reduce_fusion.6, f32[2,288]{1,0:T(2,128)S(1)} %pad_maximum_fusion.3, f32[1152]{0:T(1024)S(1)} %copy-done.42, ...), channel_id=1, replica_groups=mesh['dp'=8,'tensor'=4] {'dp'}, use_global_device_ids=true, to_apply=%region_25.26 | all-reduce | flops 5760 | bytes 46080 | tf_op jit(solution)/shard_map/psum | solution.py:188
  1638.2 128.6 %all-reduce.14.cloned.1.call-done = (f32[1000,1152]{1,0:T(8,128)}, f32[1001,1152]{1,0:T(8,128)}) async-done(((f32[1000,1152]{1,0:T(8,128)}, f32[1001,1152]{1,0:T(8,128)}), (f32[1000,1152]{1,0:T(8,128)}, f32[1001,1152]{1,0:T(8,128)})) %all-reduce.14.cloned.1.call-update) | async-done | bytes 9220624 | tf_op jit(solution)/shard_map/psum | solution.py:205
  1766.7 300.5 %all-reduce.16.cloned.1.call-done = (f32[1152,6,288]{0,2,1:T(8,128)}, f32[1152,3,288]{0,2,1:T(8,128)}, f32[288,1152]{1,0:T(8,128)}, f32[1152,1152]{1,0:T(8,128)}, f32[1152,1152]{1,0:T(8,128)}) async-done(((f32[1152,6,288]{0,2,1:T(8,128)}, f32[1152,3,288]{0,2,1:T(8,128)}, f32[288,1152]{1,0:T(8,128)}, f32[1152,1152]{1,0:T(8,128)}, f32[1152,1152]{1,0:T(8,128)}), (f32[1152,6,288]{0,2,1:T(8,128)}, ...) | async-done | bytes 23887888 | tf_op jit(solution)/shard_map/psum | solution.py:188
  2067.2 5.1 copy.107
  2072.3 2.4 copy.108
  2075.1 1.6 slice-done.13
  2076.8 4.0 copy.109
  2081.8 1.9 copy.110
  2083.7 1.1 copy.111
  2084.8 2.7 copy.112
  2088.0 1.5 slice-done.15
  2089.6 2.4 copy.113
  (199 shorter events, 8.8 us)
Async XLA Ops:
  7.2 509.5 %copy-start = (bf16[1152,1152]{1,0:T(8,128)(2,1)S(1)}, bf16[1152,1152]{1,0:T(8,128)(2,1)}, u32[]{:S(2)}) copy-start(bf16[1152,1152]{1,0:T(8,128)(2,1)} %param.32) | copy-start | bytes 7962628
  7.2 7.8 copy-start.46
  7.2 7.9 copy-start.50
  7.2 8.3 copy-start.52
  7.2 483.1 %all-reduce.10.cloned.1.call-start = ((), (), s32[]{:S(2)}) async-start(), calls=%async_computation | async-start | bytes 18874368 | tf_op jit(solution)/shard_map/psum | solution.py:100
  7.3 7.8 copy-start.15
  7.3 8.3 copy-start.14
  7.3 9.4 copy-start.6
  10.5 128.8 %copy-start.32 = (f32[8,256]{1,0:T(8,128)}, f32[8,256]{1,0:T(8,128)S(1)}, u32[]{:S(2)}) copy-start(f32[8,256]{1,0:T(8,128)S(1)} %broadcast_multiply_fusion.5) | copy-start | bytes 24580
  15.0 124.3 %copy-start.34 = (f32[8,256]{1,0:T(8,128)}, f32[8,256]{1,0:T(8,128)S(1)}, u32[]{:S(2)}) copy-start(f32[8,256]{1,0:T(8,128)S(1)} %add_rsqrt_fusion.1) | copy-start | bytes 24580
  135.9 11.2 copy-start.38
  139.3 7.9 copy-start.28
  151.1 5.2 copy-start.44
  151.2 5.2 copy-start.9
  159.6 6.1 copy-start.47
  159.6 6.1 copy-start.48
  165.0 700.2 %all-reduce.12.cloned.1.call-start = ((), (), s32[]{:S(2)}) async-start(), calls=%async_computation.1 | async-start | bytes 18874368 | tf_op jit(solution)/shard_map/psum | solution.py:125
  165.7 324.6 %copy-start.36 = (f32[1152]{0:T(1024)}, f32[1152]{0:T(1024)S(1)}, u32[]{:S(2)}) copy-start(f32[1152]{0:T(1024)S(1)} %convert_element_type.142) | copy-start | bytes 13828
  180.0 336.7 %copy-start.54 = (f32[8]{0:T(128)}, f32[8]{0:T(128)S(1)}, u32[]{:S(2)}) copy-start(f32[8]{0:T(128)S(1)} %compare_convert_fusion) | copy-start | bytes 100
  490.3 15.3 copy-start.57
  500.7 6.4 copy-start.2
  500.7 6.4 copy-start.40
  500.7 15.9 slice-start.10
  507.1 9.6 slice-start.11
  541.5 995.5 %all-reduce.18.cloned.1.call-start = ((), (), s32[]{:S(2)}) async-start(), calls=%async_computation.4 | async-start | bytes 37748736 | tf_op jit(solution)/shard_map/psum | solution.py:110
  555.3 318.4 %copy-start.55 = (f32[8]{0:T(128)S(1)}, f32[8]{0:T(128)}, u32[]{:S(2)}) copy-start(f32[8]{0:T(128)} %copy-done.54) | copy-start | bytes 100
  865.2 9.2 copy-start.4
  885.8 5.2 slice-start.1
  887.6 5.2 copy-start.10
  887.6 5.2 copy-start.45
  892.8 7.6 copy-start.19
  900.4 8.0 copy-start.23
  908.4 858.3 %all-reduce.14.cloned.1.call-start = ((), (), s32[]{:S(2)}) async-start(), calls=%async_computation.2 | async-start | bytes 18505728 | tf_op jit(solution)/shard_map/psum | solution.py:205
  909.1 627.9 %copy-start.29 = (f32[8,1152]{1,0:T(8,128)S(1)}, f32[8,1152]{1,0:T(8,128)}, u32[]{:S(2)}) copy-start(f32[8,1152]{1,0:T(8,128)} %copy-done.28) | copy-start | bytes 110596
  909.1 627.9 %copy-start.33 = (f32[8,256]{1,0:T(8,128)S(1)}, f32[8,256]{1,0:T(8,128)}, u32[]{:S(2)}) copy-start(f32[8,256]{1,0:T(8,128)} %copy-done.32) | copy-start | bytes 24580
  909.1 627.9 %copy-start.35 = (f32[8,256]{1,0:T(8,128)S(1)}, f32[8,256]{1,0:T(8,128)}, u32[]{:S(2)}) copy-start(f32[8,256]{1,0:T(8,128)} %copy-done.34) | copy-start | bytes 24580
  1537.0 22.2 %slice-start.2 = ((s8[4718592]{0:T(1024)(128)(4,1)}), s8[4194304]{0:T(1024)(128)(4,1)S(1)}, s32[]{:S(2)}) async-start(s8[4718592]{0:T(1024)(128)(4,1)} %bitcast.124), calls=%async_computation.7 | async-start | bytes 8388608
  1537.0 22.2 %slice-start.4 = ((s8[9437184]{0:T(1024)(128)(4,1)}), s8[4194304]{0:T(1024)(128)(4,1)S(1)}, s32[]{:S(2)}) async-start(s8[9437184]{0:T(1024)(128)(4,1)} %bitcast.126), calls=%async_computation.9 | async-start | bytes 8388608
  1537.0 22.2 %slice-start.5 = ((s8[9437184]{0:T(1024)(128)(4,1)}), s8[4194304]{0:T(1024)(128)(4,1)S(1)}, s32[]{:S(2)}) async-start(s8[9437184]{0:T(1024)(128)(4,1)} %bitcast.126), calls=%async_computation.10 | async-start | bytes 8388608
  1537.0 22.2 %slice-start.7 = ((s8[9437184]{0:T(1024)(128)(4,1)}), s8[4194304]{0:T(1024)(128)(4,1)S(1)}, s32[]{:S(2)}) async-start(s8[9437184]{0:T(1024)(128)(4,1)} %bitcast.128), calls=%async_computation.12 | async-start | bytes 8388608
  1537.0 22.2 %slice-start.8 = ((s8[9437184]{0:T(1024)(128)(4,1)}), s8[4194304]{0:T(1024)(128)(4,1)S(1)}, s32[]{:S(2)}) async-start(s8[9437184]{0:T(1024)(128)(4,1)} %bitcast.128), calls=%async_computation.13 | async-start | bytes 8388608
  1545.9 13.3 slice-start.3
  1545.9 13.3 slice-start.6
  1545.9 13.3 slice-start.9
  1545.9 13.3 copy-start.37
  1559.3 9.2 copy-start.7
  1559.3 9.2 copy-start.27
  1559.3 9.9 copy-start.51
  1568.4 5.2 copy-start.53
  1569.2 9.2 copy-start.41
  1577.9 15.6 copy-start.18
  1577.9 489.3 %all-reduce.16.cloned.1.call-start = ((), (), s32[]{:S(2)}) async-start(), calls=%async_computation.3 | async-start | bytes 47775744 | tf_op jit(solution)/shard_map/psum | solution.py:188
  1593.5 5.3 copy-start.20
  1593.5 5.3 copy-start.22
  1593.5 5.3 copy-start.24
  1593.5 5.3 copy-start.39
  2067.2 5.1 copy-start.12
  2067.2 7.9 slice-start.12
  2072.3 12.5 slice-start.16
  2076.8 5.0 copy-start.13
  2076.8 7.0 copy-start.16
  2076.8 8.0 slice-start.17
  2083.7 8.2 copy-start.1
  2084.8 4.7 slice-start.15
  (19 other events, 42.5 us)
Sparse Core Ops, SparseCore 0:
  165.1 325.1 all-reduce.9
  541.6 323.5 all-reduce.11
  908.5 628.3 all-reduce.17
  1578.0 188.6 all-reduce.13
  1772.5 294.6 all-reduce.15
where the time goes:
time: 2100 us
  waiting for transfers between devices  1660 us (79%)
  matrix products  144 us (7%)
  blocking collectives  115 us (5%)
  local copies, waits for them, and re-layouts  84.7 us (4%)
  other arithmetic  78.3 us (4%)
    psum x1, waiting for transfers between devices, local(): branch = lax.psum(mlp_part, 'tensor') + down_bias.astype(wide)  611 us
    psum x1, waiting for transfers between devices, local(): attention = lax.psum(attn_part, 'tensor') + proj_bias.astype(wide)  310 us
    psum x1, waiting for transfers between devices, local(): d_hidden_mlp = lax.psum(d_mlp_part, 'tensor')  310 us
    psum x1, waiting for transfers between devices, local(): lax.psum((grad_qkv_weight, grad_qv_bias, grad_proj_weight, grad_proj_bias...  300 us
    psum x1, waiting for transfers between devices, local(): lax.psum((grad_time_table, grad_class_table), ('dp', 'tensor'))  129 us
    all_gather x1, blocking collectives, local(): modulation = lax.all_gather(mod_local, 'tensor', axis=2, tiled=True)  91.1 us
    unnamed x174, local copies, waits for them, and re-layouts  57 us
  transfers between devices with their start and end apart: 5, of which 5 were waited for; matrix products, arithmetic and copies ran while one was open for 4% of the time, Pallas kernels for 0%

commit v1 on v0

--- a/solution.py
+++ b/solution.py
@@ -122,7 +122,11 @@
         (grad_down_weight, grad_down_bias, grad_up_weight, grad_up_bias), "dp"
     )
     d_mlp_part = jnp.einsum("gsf,df->gsd", d_pre, up_weight, preferred_element_type=wide)
-    d_hidden_mlp = lax.psum(d_mlp_part, "tensor")
+    d_hidden_mlp = d_mlp_part
+    for hop in (1, 2):
+        d_hidden_mlp = d_hidden_mlp + lax.ppermute(
+            d_hidden_mlp, "tensor", [(dev, dev ^ hop) for dev in range(4)]
+        )
     d_shift_mlp = jnp.sum(d_hidden_mlp, axis=1)
     d_scale_mlp = jnp.sum(d_hidden_mlp * normed_mlp, axis=1)
     d_middle = grad_out + norm_back(d_hidden_mlp * (1.0 + scale_mlp), normed_mlp, inverse_mlp)

time: 2100 us -> 2390 us (1.14)
  waiting for transfers between devices: 1660 us -> 1950 us
    ppermute x0 -> x2, waiting for transfers between devices: none -> 593 us  [local(): lax.ppermute(d_hidden_mlp, 'tensor', [(dev, dev ^ hop) for dev in range(4)])]
    psum x1 -> x0, waiting for transfers between devices: 310 us -> none  [local(): d_hidden_mlp = lax.psum(d_mlp_part, 'tensor')]
    unnamed x174 -> x178, local copies, waits for them, and re-layouts: 57 us -> 53.4 us
  transfers between devices with their start and end apart: 5 -> 6, of which waited for: 5 -> 6; matrix products, arithmetic and copies ran while one was open for 4% -> 3% of each run, Pallas kernels for 0% -> 0%
where the time goes in v1:
time: 2390 us
  waiting for transfers between devices  1950 us (82%)
  matrix products  144 us (6%)
  blocking collectives  115 us (5%)
  other arithmetic  86.7 us (4%)
  local copies, waits for them, and re-layouts  81.1 us (3%)
    psum x1, waiting for transfers between devices, local(): branch = lax.psum(mlp_part, 'tensor') + down_bias.astype(wide)  612 us
    ppermute x2, waiting for transfers between devices, local(): lax.ppermute(d_hidden_mlp, 'tensor', [(dev, dev ^ hop) for dev in range(4)])  593 us
    psum x1, waiting for transfers between devices, local(): attention = lax.psum(attn_part, 'tensor') + proj_bias.astype(wide)  311 us
    psum x1, waiting for transfers between devices, local(): lax.psum((grad_qkv_weight, grad_qv_bias, grad_proj_weight, grad_proj_bias...  301 us
    psum x1, waiting for transfers between devices, local(): lax.psum((grad_time_table, grad_class_table), ('dp', 'tensor'))  129 us
    all_gather x1, blocking collectives, local(): modulation = lax.all_gather(mod_local, 'tensor', axis=2, tiled=True)  90.6 us
    unnamed x178, local copies, waits for them, and re-layouts  53.4 us
  transfers between devices with their start and end apart: 6, of which 6 were waited for; matrix products, arithmetic and copies ran while one was open for 3% of the time, Pallas kernels for 0%

profile of v1, /device:TPU:0, one launch (start us, length us, event | category | flops | bytes accessed | tf_op | source)
XLA Modules:
  0.0 2390.0 jit_solution(13938781230262972079)
XLA Ops:
  7.3 3.2 convert_reduce_fusion
  10.5 4.5 fusion.14
  16.6 1.3 convolution_add_fusion.1
  18.0 1.5 copy.58
  19.4 90.6 %all_gather.3 = f32[8,6,1152]{1,0,2:T(8,128)} all-gather(f32[8,6,288]{1,0,2:T(8,128)} %copy.58), channel_id=1, replica_groups=mesh['dp'=8,'tensor'=4] {'tensor'}, dimensions={2}, use_global_device_ids=true | all-gather | bytes 276480 | tf_op jit(solution)/shard_map/all_gather | solution.py:73
  110.1 22.1 fusion.73
  132.1 3.3 copy.86
  135.5 3.3 copy.85
  138.9 7.8 fusion.40
  146.7 1.1 slice.59
  147.9 2.7 fusion.72
  150.7 3.5 multiply_reduce_fusion.8
  154.3 1.6 fusion.22
  155.9 2.2 fusion.42
  158.1 1.0 copy-done.17
  159.1 5.5 fusion.49
  165.4 3.3 copy.87
  168.7 3.6 copy.88
  172.4 3.3 copy.84
  175.7 3.3 copy.89
  179.1 310.9 %all-reduce.9.cloned.1.call-done = f32[8,256,1152]{2,1,0:T(8,128)} async-done(((f32[8,256,1152]{2,1,0:T(8,128)}), f32[8,256,1152]{2,1,0:T(8,128)}) %all-reduce.9.cloned.1.call-update) | async-done | bytes 9437200 | tf_op jit(solution)/shard_map/psum | solution.py:100
  490.0 10.4 fusion.71
  500.4 4.9 multiply_reduce_fusion.4
  505.3 1.4 copy-done.2
  506.8 9.6 fusion.35
  516.4 13.2 convert_reduce_fusion.2
  529.6 7.1 fusion.33
  536.8 3.6 copy-done.9
  540.3 201.0 %collective-permute-done = f32[8,256,1152]{2,1,0:T(8,128)} collective-permute-done((f32[8,256,1152]{2,1,0:T(8,128)S(1)}, f32[8,256,1152]{2,1,0:T(8,128)}, u32[]{:S(2)}, u32[]{:S(2)}) %collective-permute-start) | collective-permute-done | bytes 9437216 | tf_op jit(solution)/shard_map/ppermute | solution.py:127
  741.3 11.0 add.213
  752.4 1.4 collective-permute-start.1
  753.8 13.3 fusion.31
  767.1 392.3 %collective-permute-done.1 = f32[8,256,1152]{2,1,0:T(8,128)} collective-permute-done((f32[8,256,1152]{2,1,0:T(8,128)}, f32[8,256,1152]{2,1,0:T(8,128)}, u32[]{:S(2)}, u32[]{:S(2)}) %collective-permute-start.1) | collective-permute-done | bytes 9437216 | tf_op jit(solution)/shard_map/ppermute | solution.py:127
  1159.5 9.2 multiply_reduce_fusion.1
  1168.7 8.1 convert_reduce_fusion.3
  1176.8 4.2 convolution_convert_fusion
  1181.7 1.8 convert_reduce_fusion.4
  1183.5 2.6 multiply_reduce_fusion.5
  1186.1 2.2 multiply_convert_fusion.4
  1188.4 1.4 multiply_convert_fusion.5
  1190.9 8.0 convolution_bitcast_fusion.2
  1199.5 16.2 convolution_bitcast_fusion
  1215.7 612.2 %all-reduce.15.cloned.1.call-done = (f32[8,256,1152]{2,1,0:T(8,128)}, f32[8,256,1152]{2,1,0:T(8,128)}) async-done(((f32[8,256,1152]{2,1,0:T(8,128)}, f32[8,256,1152]{2,1,0:T(8,128)}), (f32[8,256,1152]{2,1,0:T(8,128)}, f32[8,256,1152]{2,1,0:T(8,128)})) %all-reduce.15.cloned.1.call-update) | async-done | bytes 18874384 | tf_op jit(solution)/shard_map/psum | solution.py:110
  1828.0 9.1 fusion.13
  1837.2 13.2 convert_reduce_fusion.1
  1850.6 9.1 multiply_reduce_fusion.2
  1860.5 4.4 fusion.54
  1864.9 4.3 fusion.53
  1869.4 15.0 convolution_bitcast_fusion.1
  1884.5 5.3 convolution_bitcast_fusion.4
  1889.8 9.9 convolution_bitcast_fusion.3
  1899.7 4.7 fusion.56
  1905.1 24.3 %all-reduce.1 = (f32[6,288]{1,0:T(8,128)}, f32[2,288]{1,0:T(2,128)}, f32[1152]{0:T(1024)}, f32[1152]{0:T(1024)}, f32[1152]{0:T(1024)}) all-reduce(f32[6,288]{1,0:T(8,128)S(1)} %convert_reduce_fusion.6, f32[2,288]{1,0:T(2,128)S(1)} %pad_maximum_fusion.3, f32[1152]{0:T(1024)S(1)} %copy-done.41, ...), channel_id=1, replica_groups=mesh['dp'=8,'tensor'=4] {'dp'}, use_global_device_ids=true, to_apply=%region_24.25 | all-reduce | flops 5760 | bytes 46080 | tf_op jit(solution)/shard_map/psum | solution.py:192
  1929.3 128.7 %all-reduce.11.cloned.1.call-done = (f32[1000,1152]{1,0:T(8,128)}, f32[1001,1152]{1,0:T(8,128)}) async-done(((f32[1000,1152]{1,0:T(8,128)}, f32[1001,1152]{1,0:T(8,128)}), (f32[1000,1152]{1,0:T(8,128)}, f32[1001,1152]{1,0:T(8,128)})) %all-reduce.11.cloned.1.call-update) | async-done | bytes 9220624 | tf_op jit(solution)/shard_map/psum | solution.py:209
  2058.0 300.5 %all-reduce.13.cloned.1.call-done = (f32[1152,6,288]{0,2,1:T(8,128)}, f32[1152,3,288]{0,2,1:T(8,128)}, f32[288,1152]{1,0:T(8,128)}, f32[1152,1152]{1,0:T(8,128)}, f32[1152,1152]{1,0:T(8,128)}) async-done(((f32[1152,6,288]{0,2,1:T(8,128)}, f32[1152,3,288]{0,2,1:T(8,128)}, f32[288,1152]{1,0:T(8,128)}, f32[1152,1152]{1,0:T(8,128)}, f32[1152,1152]{1,0:T(8,128)}), (f32[1152,6,288]{0,2,1:T(8,128)}, ...) | async-done | bytes 23887888 | tf_op jit(solution)/shard_map/psum | solution.py:192
  2358.5 5.1 copy.106
  2363.6 2.4 copy.107
  2366.4 1.6 slice-done.18
  2368.0 4.0 copy.108
  2373.1 1.9 copy.109
  2375.0 1.1 copy.110
  2376.1 2.7 copy.111
  2379.3 1.5 slice-done.20
  2380.8 2.4 copy.112
  (207 shorter events, 8.2 us)
Async XLA Ops:
  7.2 509.2 %copy-start = (bf16[1152,1152]{1,0:T(8,128)(2,1)S(1)}, bf16[1152,1152]{1,0:T(8,128)(2,1)}, u32[]{:S(2)}) copy-start(bf16[1152,1152]{1,0:T(8,128)(2,1)} %param.32) | copy-start | bytes 7962628
  7.2 7.8 copy-start.45
  7.2 7.9 copy-start.49
  7.2 8.3 copy-start.51
  7.2 482.7 %all-reduce.9.cloned.1.call-start = ((), (), s32[]{:S(2)}) async-start(), calls=%async_computation | async-start | bytes 18874368 | tf_op jit(solution)/shard_map/psum | solution.py:100
  7.3 7.8 copy-start.15
  7.3 8.3 copy-start.14
  7.3 9.4 copy-start.6
  10.5 128.3 %copy-start.31 = (f32[8,256]{1,0:T(8,128)}, f32[8,256]{1,0:T(8,128)S(1)}, u32[]{:S(2)}) copy-start(f32[8,256]{1,0:T(8,128)S(1)} %broadcast_multiply_fusion.5) | copy-start | bytes 24580
  15.0 123.8 %copy-start.33 = (f32[8,256]{1,0:T(8,128)}, f32[8,256]{1,0:T(8,128)S(1)}, u32[]{:S(2)}) copy-start(f32[8,256]{1,0:T(8,128)S(1)} %add_rsqrt_fusion.1) | copy-start | bytes 24580
  135.5 11.2 copy-start.37
  138.8 7.9 copy-start.29
  150.7 5.2 copy-start.42
  150.7 5.2 copy-start.10
  159.1 6.2 copy-start.46
  159.1 6.2 copy-start.47
  164.6 1663.3 %all-reduce.15.cloned.1.call-start = ((), (), s32[]{:S(2)}) async-start(), calls=%async_computation.3 | async-start | bytes 37748736 | tf_op jit(solution)/shard_map/psum | solution.py:110
  165.4 324.6 %copy-start.35 = (f32[1152]{0:T(1024)}, f32[1152]{0:T(1024)S(1)}, u32[]{:S(2)}) copy-start(f32[1152]{0:T(1024)S(1)} %convert_element_type.142) | copy-start | bytes 13828
  179.0 326.3 %copy-start.39 = (f32[8,1,1152]{2,0,1:T(8,128)}, f32[8,1,1152]{2,0,1:T(8,128)S(1)}, u32[]{:S(2)}) copy-start(f32[8,1,1152]{2,0,1:T(8,128)S(1)} %copy.89) | copy-start | bytes 110596
  490.0 15.4 copy-start.54
  500.4 6.4 copy-start.2
  500.4 15.9 slice-start.13
  506.8 9.6 slice-start.14
  529.6 7.1 copy-start.56
  536.7 204.7 %collective-permute-start = (f32[8,256,1152]{2,1,0:T(8,128)S(1)}, f32[8,256,1152]{2,1,0:T(8,128)}, u32[]{:S(2)}, u32[]{:S(2)}) collective-permute-start(f32[8,256,1152]{2,1,0:T(8,128)S(1)} %fusion.33), channel_id=1, source_target_pairs={{0,1},{1,0},{2,3},{3,2},{4,5},{5,4},{6,7},{7,6},{8,9},{9,8},{10,11... | collective-permute-start | bytes 28311560 | tf_op jit(solution)/shard_map/ppermute | solution.py:127
  741.3 427.3 %slice-start.15 = ((s8[4718592]{0:T(1024)(128)(4,1)}), s8[524288]{0:T(1024)(128)(4,1)S(1)}, s32[]{:S(2)}) async-start(s8[4718592]{0:T(1024)(128)(4,1)} %bitcast.136), calls=%async_computation.19 | async-start | bytes 1048576
  752.4 407.1 %collective-permute-start.1 = (f32[8,256,1152]{2,1,0:T(8,128)}, f32[8,256,1152]{2,1,0:T(8,128)}, u32[]{:S(2)}, u32[]{:S(2)}) collective-permute-start(f32[8,256,1152]{2,1,0:T(8,128)} %add.213), channel_id=1, source_target_pairs={{0,2},{1,3},{2,0},{3,1},{4,6},{5,7},{6,4},{7,5},{8,10},{9,11},{10,... | collective-permute-start | bytes 28311560 | tf_op jit(solution)/shard_map/ppermute | solution.py:127
  753.8 405.7 %copy-start.4 = (f32[8,256,1152]{2,1,0:T(8,128)S(1)}, f32[8,256,1152]{2,1,0:T(8,128)}, u32[]{:S(2)}) copy-start(f32[8,256,1152]{2,1,0:T(8,128)} %add.213) | copy-start | bytes 28311556
  753.8 414.9 %slice-start = ((s8[9437184]{0:T(1024)(128)(4,1)}), s8[4194304]{0:T(1024)(128)(4,1)S(1)}, s32[]{:S(2)}) async-start(s8[9437184]{0:T(1024)(128)(4,1)} %bitcast.122), calls=%async_computation.4 | async-start | bytes 8388608
  753.8 414.9 %slice-start.1 = ((s8[9437184]{0:T(1024)(128)(4,1)}), s8[1048576]{0:T(1024)(128)(4,1)S(1)}, s32[]{:S(2)}) async-start(s8[9437184]{0:T(1024)(128)(4,1)} %bitcast.122), calls=%async_computation.5 | async-start | bytes 2097152
  753.8 414.9 %slice-start.16 = ((s8[4718592]{0:T(1024)(128)(4,1)}), s8[4194304]{0:T(1024)(128)(4,1)S(1)}, s32[]{:S(2)}) async-start(s8[4718592]{0:T(1024)(128)(4,1)} %bitcast.136), calls=%async_computation.20 | async-start | bytes 8388608
  767.1 401.6 %slice-start.2 = ((s8[9437184]{0:T(1024)(128)(4,1)}), s8[4194304]{0:T(1024)(128)(4,1)S(1)}, s32[]{:S(2)}) async-start(s8[9437184]{0:T(1024)(128)(4,1)} %bitcast.122), calls=%async_computation.6 | async-start | bytes 8388608
  1168.7 8.1 copy-start.26
  1183.5 7.4 copy-start.19
  1190.8 8.0 copy-start.23
  1198.8 859.1 %all-reduce.11.cloned.1.call-start = ((), (), s32[]{:S(2)}) async-start(), calls=%async_computation.1 | async-start | bytes 18505728 | tf_op jit(solution)/shard_map/psum | solution.py:209
  1199.5 628.4 %copy-start.30 = (f32[8,1152]{1,0:T(8,128)S(1)}, f32[8,1152]{1,0:T(8,128)}, u32[]{:S(2)}) copy-start(f32[8,1152]{1,0:T(8,128)} %copy-done.29) | copy-start | bytes 110596
  1199.5 628.4 %copy-start.32 = (f32[8,256]{1,0:T(8,128)S(1)}, f32[8,256]{1,0:T(8,128)}, u32[]{:S(2)}) copy-start(f32[8,256]{1,0:T(8,128)} %copy-done.31) | copy-start | bytes 24580
  1199.5 628.4 %copy-start.34 = (f32[8,256]{1,0:T(8,128)S(1)}, f32[8,256]{1,0:T(8,128)}, u32[]{:S(2)}) copy-start(f32[8,256]{1,0:T(8,128)} %copy-done.33) | copy-start | bytes 24580
  1828.0 22.5 slice-start.5
  1828.0 22.5 slice-start.7
  1828.0 22.5 slice-start.8
  1828.0 22.5 slice-start.10
  1828.0 22.5 slice-start.11
  1837.1 13.3 slice-start.6
  1837.2 13.3 slice-start.9
  1837.2 13.3 slice-start.12
  1837.2 13.3 copy-start.36
  1850.5 9.2 copy-start.7
  1850.5 9.2 copy-start.28
  1850.6 9.9 copy-start.50
  1859.7 5.2 copy-start.52
  1860.5 9.0 copy-start.40
  1869.2 15.3 copy-start.18
  1869.2 489.3 %all-reduce.13.cloned.1.call-start = ((), (), s32[]{:S(2)}) async-start(), calls=%async_computation.2 | async-start | bytes 47775744 | tf_op jit(solution)/shard_map/psum | solution.py:192
  1884.5 5.3 copy-start.20
  1884.5 5.3 copy-start.22
  1884.5 5.3 copy-start.24
  1884.5 5.3 copy-start.38
  2358.5 7.9 slice-start.17
  2363.6 12.5 slice-start.21
  2368.0 7.0 copy-start.16
  2368.0 8.0 slice-start.22
  2375.0 8.2 copy-start.1
  (22 other events, 63.0 us)
Sparse Core Ops, SparseCore 0:
  164.8 325.1 all-reduce.8
  1199.0 628.9 all-reduce.14
  1869.3 188.6 all-reduce.10
  2063.7 294.7 all-reduce.12
